TPU v7x, 256 devices: a whole 4x4x8 slice. The times are simulated.
256 devices in a mesh: probe: 4 (over y_lo, core), tile: 32 (over z, x), level: 2 (over y_hi).
Axes of the slice: x: 4, y: 4 (y_hi: 2, y_lo: 2; y = y_hi * 2 + y_lo), z: 8, core: 2. Of those that a mesh axis runs over, the one named last changes fastest.
Arguments:
- probe_bits: int32 [4, 64, 256, 256], P('probe', 'level', 'tile'), may hold values from 0 to 1
- kappa_sq: float32 [64, 256, 256], P('level', 'tile'), may hold values from 0.25 to 4
- observed: float32 [64, 256, 256], P('level', 'tile'), may hold values from -0.6 to 0.6
Outputs:
- gradient: float32 [64, 256, 256], P('level', 'tile', 'probe')
Inputs may be any that keep to these rules, and one draw needn't show every extreme that they name: `probe_bits`: a probe's sign is 2 times its bit minus 1.
All inputs are finite; a program needn't handle non-finite values.
Results may differ from a plain program's by a relative error of at most 0.0003.
Values sent between devices are 32-bit elements; how exact they have to be, the bound alone decides.
A program may use at most 64 MiB of HBM per device.

v0:
```python
import jax
import jax.numpy as jnp
from jax import lax
from jax.sharding import PartitionSpec as P

ITERS = 4
VERTICAL = 2.0


def with_halo(cells, sides, width):
    for axis, dim in sides:
        count = lax.axis_size(axis)
        ends = count - 1
        head = lax.slice_in_dim(cells, 0, width, axis=dim)
        tail = lax.slice_in_dim(cells, cells.shape[dim] - width, cells.shape[dim], axis=dim)
        cells = jnp.concatenate(
            [
                lax.ppermute(tail, axis, [(i, (i + 1) % count) for i in range(ends)]),
                cells,
                lax.ppermute(head, axis, [((i + 1) % count, i) for i in range(ends)]),
            ],
            axis=dim,
        )
    return cells


def shift_levels(values, stride, level_dim, fill_value):
    level_count = values.shape[level_dim]
    widths = [(0, 0)] * values.ndim
    if stride > 0:
        widths[level_dim] = (stride, 0)
        padded = jnp.pad(values, widths, constant_values=fill_value)
        return lax.slice_in_dim(padded, 0, level_count, axis=level_dim)
    widths[level_dim] = (0, -stride)
    padded = jnp.pad(values, widths, constant_values=fill_value)
    return lax.slice_in_dim(padded, -stride, level_count - stride, axis=level_dim)


def reduction_tables(kappa_sq):
    level_count = kappa_sq.shape[0]
    level_ids = lax.broadcasted_iota(jnp.int32, kappa_sq.shape, 0)
    diagonal = kappa_sq + (4.0 + 2.0 * VERTICAL)
    lower = jnp.where(level_ids > 0, -VERTICAL, 0.0).astype(jnp.float32)
    upper = jnp.where(level_ids < level_count - 1, -VERTICAL, 0.0).astype(jnp.float32)
    tables = []
    stride = 1
    while stride < level_count:
        lower_ratio = -lower / shift_levels(diagonal, stride, 0, 1.0)
        upper_ratio = -upper / shift_levels(diagonal, -stride, 0, 1.0)
        new_diagonal = (
            diagonal
            + lower_ratio * shift_levels(upper, stride, 0, 0.0)
            + upper_ratio * shift_levels(lower, -stride, 0, 0.0)
        )
        new_lower = lower_ratio * shift_levels(lower, stride, 0, 0.0)
        upper = upper_ratio * shift_levels(upper, -stride, 0, 0.0)
        lower = new_lower
        diagonal = new_diagonal
        tables.append((lower_ratio, upper_ratio, stride))
        stride = stride * 2
    return (tables, 1.0 / diagonal)


def vertical_solve(values, tables, inverse_diagonal):
    for lower_ratio, upper_ratio, stride in tables:
        values = (
            values
            + lower_ratio * shift_levels(values, stride, 1, 0.0)
            + upper_ratio * shift_levels(values, -stride, 1, 0.0)
        )
    return values * inverse_diagonal


def stencil(padded, values, kappa_sq):
    beside_x = padded[:, 1:-1, 2:, 1:-1] + padded[:, 1:-1, :-2, 1:-1]
    beside_y = padded[:, 1:-1, 1:-1, 2:] + padded[:, 1:-1, 1:-1, :-2]
    beside_z = padded[:, 2:, 1:-1, 1:-1] + padded[:, :-2, 1:-1, 1:-1]
    return (kappa_sq + (4.0 + 2.0 * VERTICAL)) * values - beside_x - beside_y - VERTICAL * beside_z


def slab_apply(values, kappa_sq):
    extended = with_halo(values, (("tile", 2), ("level", 1)), 1)
    padded = jnp.pad(extended, ((0, 0), (0, 0), (0, 0), (1, 1)))
    return stencil(padded, values, kappa_sq)


def local_dots(first, second):
    return jnp.sum(first * second, axis=(1, 2, 3))


def precond_total(residual, precond):
    return lax.psum(local_dots(residual, precond), ("tile", "level"))


def conjugate_solve(right_side, apply_q, apply_m):
    shaped = (right_side.shape[0], 1, 1, 1)
    solution = jnp.zeros_like(right_side)
    residual = right_side
    precond = apply_m(residual)
    rho_now = precond_total(residual, precond)
    direction = precond
    for iteration in range(ITERS):
        image_field = apply_q(direction)
        curv_total = lax.psum(local_dots(direction, image_field), ("tile", "level"))
        step_size = (rho_now / curv_total).reshape(shaped)
        solution = solution + step_size * direction
        if iteration + 1 < ITERS:
            residual = residual - step_size * image_field
            precond = apply_m(residual)
            rho_next = precond_total(residual, precond)
            direction = precond + (rho_next / rho_now).reshape(shaped) * direction
            rho_now = rho_next
    return solution


def body(probe_bits, kappa_sq, observed):
    sign_field = (2 * probe_bits - 1).astype(jnp.float32)
    stacked = jnp.concatenate([sign_field, observed[None]], axis=0)
    extended = with_halo(stacked, (("tile", 2), ("level", 1)), 1)
    padded = jnp.pad(extended, ((0, 0), (0, 0), (0, 0), (1, 1)))
    k_stacked = stencil(padded, stacked, kappa_sq)
    k_signs = k_stacked[:-1]
    data_term = 2.0 * observed * k_stacked[-1]
    kappa_cols = lax.all_to_all(kappa_sq[None], "level", split_axis=3, concat_axis=1, tiled=True)[0]
    tables, inverse_diagonal = reduction_tables(kappa_cols)

    def solve_columns(columns):
        solved = vertical_solve(
            vertical_solve(columns, tables, inverse_diagonal), tables, inverse_diagonal
        )
        return lax.all_to_all(solved, "level", split_axis=1, concat_axis=3, tiled=True)

    def apply_m(values):
        return solve_columns(
            lax.all_to_all(values, "level", split_axis=3, concat_axis=1, tiled=True)
        )

    def apply_q(values):
        return slab_apply(slab_apply(values, kappa_sq), kappa_sq)

    solution = conjugate_solve(sign_field, apply_q, apply_m)
    probe_partial = jnp.sum(
        solution * k_signs + slab_apply(solution, kappa_sq) * sign_field, axis=0
    )
    summed = lax.psum_scatter(probe_partial, "probe", scatter_dimension=2, tiled=True)
    y_width = summed.shape[2]
    offset = lax.axis_index("probe") * y_width
    kappa_part = lax.dynamic_slice_in_dim(kappa_sq, offset, y_width, 2)
    data_part = lax.dynamic_slice_in_dim(data_term, offset, y_width, 2)
    probe_count = probe_bits.shape[0] * lax.axis_size("probe")
    return kappa_part * (summed / probe_count - data_part)


def solution(mesh):
    in_specs = (
        P("probe", "level", "tile", None),
        P("level", "tile", None),
        P("level", "tile", None),
    )
    out_specs = P("level", "tile", "probe")
    return jax.shard_map(body, mesh=mesh, in_specs=in_specs, out_specs=out_specs, check_vma=False)
```

profile of v0, /device:TPU:1, one launch (start us, length us, event | category | flops | bytes accessed | tf_op | source)
XLA Modules:
  0.0 1670.7 jit_solution(17637381411247329690)
XLA Ops:
  9.1 5.0 all-to-all-start.1
  33.5 8.0 all_to_all.165
  51.2 4.7 collective-permute-done.3
  58.1 4.3 collective-permute-start.5
  66.3 4.7 collective-permute-done.7
  73.2 158.1 %all-reduce.140 = (f32[1]{0:T(128)}, f32[1]{0:T(128)}) all-reduce(f32[1]{0:T(128)} %bitcast.26, f32[1]{0:T(128)} %bitcast.30), channel_id=1, replica_groups=mesh['probe'=4,'tile'=32,'level'=2] {'tile','level'}, use_global_device_ids=true, to_apply=%region_1.2 | all-reduce | flops 2 | bytes 16 | tf_op jit(solution)/shard_map/psum | solution.py:92
  239.0 9.9 all_to_all.166
  259.4 8.0 all_to_all.167
  268.1 149.1 %psum.58 = f32[1]{0:T(128)} all-reduce(f32[1]{0:T(128)} %bitcast.39), channel_id=1, replica_groups=mesh['probe'=4,'tile'=32,'level'=2] {'tile','level'}, use_global_device_ids=true, to_apply=%region_5.6 | all-reduce | flops 1 | bytes 8 | tf_op jit(solution)/shard_map/psum | solution.py:92
  425.9 5.0 collective-permute-start.10
  432.2 5.0 collective-permute-done.11
  448.0 4.7 collective-permute-done.15
  454.8 149.1 %psum.59 = f32[1]{0:T(128)} all-reduce(f32[1]{0:T(128)} %bitcast.43), channel_id=1, replica_groups=mesh['probe'=4,'tile'=32,'level'=2] {'tile','level'}, use_global_device_ids=true, to_apply=%region_7.8 | all-reduce | flops 1 | bytes 8 | tf_op jit(solution)/shard_map/psum | solution.py:104
  611.7 10.3 all_to_all.168
  632.5 7.9 all_to_all.169
  641.7 149.8 %psum.60 = f32[1]{0:T(128)} all-reduce(f32[1]{0:T(128)} %bitcast.52), channel_id=1, replica_groups=mesh['probe'=4,'tile'=32,'level'=2] {'tile','level'}, use_global_device_ids=true, to_apply=%region_9.10 | all-reduce | flops 1 | bytes 8 | tf_op jit(solution)/shard_map/psum | solution.py:92
  800.2 4.4 collective-permute-start.18
  805.9 4.7 collective-permute-done.19
  812.8 4.3 collective-permute-start.21
  821.1 5.0 collective-permute-done.23
  828.2 149.4 %psum.61 = f32[1]{0:T(128)} all-reduce(f32[1]{0:T(128)} %bitcast.56), channel_id=1, replica_groups=mesh['probe'=4,'tile'=32,'level'=2] {'tile','level'}, use_global_device_ids=true, to_apply=%region_11.12 | all-reduce | flops 1 | bytes 8 | tf_op jit(solution)/shard_map/psum | solution.py:104
  985.3 10.2 all_to_all.170
  1006.0 8.1 all_to_all.171
  1014.8 150.4 %psum.62 = f32[1]{0:T(128)} all-reduce(f32[1]{0:T(128)} %bitcast.65), channel_id=1, replica_groups=mesh['probe'=4,'tile'=32,'level'=2] {'tile','level'}, use_global_device_ids=true, to_apply=%region_13.14 | all-reduce | flops 1 | bytes 8 | tf_op jit(solution)/shard_map/psum | solution.py:92
  1172.9 4.1 collective-permute-start.26
  1179.7 4.3 collective-permute-start.33
  1191.2 5.6 collective-permute-start.30
  1198.2 5.5 collective-permute-start.34
  1206.5 152.8 %psum.63 = f32[1]{0:T(128)} all-reduce(f32[1]{0:T(128)} %bitcast.69), channel_id=1, replica_groups=mesh['probe'=4,'tile'=32,'level'=2] {'tile','level'}, use_global_device_ids=true, to_apply=%region_15.16 | all-reduce | flops 1 | bytes 8 | tf_op jit(solution)/shard_map/psum | solution.py:104
  1376.1 4.4 copy.71
  1380.5 4.7 reshape.177
  1385.2 275.9 %reduce-scatter.4.cloned.1.call-done = f32[64,256]{1,0:T(8,128)} async-done(((f32[256,256]{1,0:T(8,128)}), f32[64,256]{1,0:T(8,128)}) %reduce-scatter.4.cloned.1.call-update) | async-done | bytes 65552
  (269 shorter events, 169.6 us)
Async XLA Ops:
  9.1 10.5 all-to-all-start.1
  19.7 9.0 all-to-all-start
  23.1 1637.9 %reduce-scatter.4.cloned.1.call-start = ((), (), s32[]{:S(2)}) async-start(), calls=%async_computation.10 | async-start | bytes 327680
  41.7 5.3 collective-permute-start
  49.9 6.0 collective-permute-start.3
  56.8 5.6 collective-permute-start.4
  58.1 5.3 collective-permute-start.5
  65.0 6.0 collective-permute-start.7
  419.5 5.3 collective-permute-start.8
  425.9 6.3 collective-permute-start.10
  430.9 6.3 collective-permute-start.11
  438.8 5.3 collective-permute-start.12
  446.7 6.0 collective-permute-start.15
  793.9 5.3 collective-permute-start.16
  800.2 5.7 collective-permute-start.18
  804.6 6.0 collective-permute-start.19
  811.5 5.6 collective-permute-start.20
  812.8 5.3 collective-permute-start.21
  819.7 6.3 collective-permute-start.23
  1166.5 5.3 collective-permute-start.24
  1172.9 11.1 collective-permute-start.26
  1177.0 7.0 collective-permute-start.27
  1178.4 19.8 %collective-permute-start.32 = (f32[2,32,1,256]{3,2,1,0:T(1,128)S(1)}, f32[2,32,1,256]{3,2,1,0:T(1,128)S(1)}, u32[]{:S(2)}, u32[]{:S(2)}) collective-permute-start(f32[2,32,1,256]{3,2,1,0:T(1,128)S(1)} %get-tuple-element.47), channel_id=1, source_target_pairs={{2,0},{4,2},{6,4},{8,6},{10,8},{12,10},{14,12},{16,14},{18,16},{20... | collective-permute-start | bytes 196616 | tf_op jit(solution)/shard_map/ppermute | solution.py:20
  1179.7 18.5 %collective-permute-start.33 = (f32[2,32,1,256]{3,2,1,0:T(1,128)S(1)}, f32[2,32,1,256]{3,2,1,0:T(1,128)S(1)}, u32[]{:S(2)}, u32[]{:S(2)}) collective-permute-start(f32[2,32,1,256]{3,2,1,0:T(1,128)S(1)} %get-tuple-element.46), channel_id=1, source_target_pairs={{0,2},{2,4},{4,6},{6,8},{8,10},{10,12},{12,14},{14,16},{16,18},{18... | collective-permute-start | bytes 196616 | tf_op jit(solution)/shard_map/ppermute | solution.py:18
  1184.9 5.3 collective-permute-start.28
  1191.2 13.8 collective-permute-start.30
  1196.9 8.2 collective-permute-start.31
  1198.2 167.8 %collective-permute-start.34 = (f32[2,1,10,256]{3,2,1,0:T(8,128)S(1)}, f32[2,1,10,256]{3,2,1,0:T(8,128)S(1)}, u32[]{:S(2)}, u32[]{:S(2)}) collective-permute-start(f32[2,1,10,256]{3,2,1,0:T(8,128)S(1)} %get-tuple-element.39), channel_id=1, source_target_pairs={{0,1},{2,3},{4,5},{6,7},{8,9},{10,11},{12,13},{14,15},{16,17},{18,... | collective-permute-start | bytes 61448 | tf_op jit(solution)/shard_map/ppermute | solution.py:18
  1203.7 162.3 %collective-permute-start.35 = (f32[2,1,10,256]{3,2,1,0:T(8,128)S(1)}, f32[2,1,10,256]{3,2,1,0:T(8,128)S(1)}, u32[]{:S(2)}, u32[]{:S(2)}) collective-permute-start(f32[2,1,10,256]{3,2,1,0:T(8,128)S(1)} %get-tuple-element.38), channel_id=1, source_target_pairs={{1,0},{3,2},{5,4},{7,6},{9,8},{11,10},{13,12},{15,14},{17,16},{19,... | collective-permute-start | bytes 61448 | tf_op jit(solution)/shard_map/ppermute | solution.py:20
  1360.7 6.3 collective-permute-start.36
  1362.0 5.0 collective-permute-start.37
  1369.0 6.1 collective-permute-start.39
  (36 other events, 1278.7 us)
Sparse Core Ops, SparseCore 0:
  1385.3 275.7 reduce-scatter.3
where the time goes:
time: 1670 us
  blocking collectives  1120 us (67%)
  waiting for transfers between devices  323 us (19%)
  starting transfers between devices  109 us (7%)
  local copies, waits for them, and re-layouts  52.3 us (3%)
  other arithmetic  41.6 us (2%)
  between operations  23.8 us (1%)
    psum x4, blocking collectives, precond_total(): return lax.psum(local_dots(residual, precond), ('tile', 'level'))  607 us
    psum x3, blocking collectives, conjugate_solve(): curv_total = lax.psum(local_dots(direction, image_field), ('tile', 'level'))  451 us
    unnamed x2, waiting for transfers between devices  276 us
    ppermute x20, starting transfers between devices, with_halo(): lax.ppermute(tail, axis, [(i, (i + 1) % count) for i in range(ends)])  74.2 us
  transfers between devices with their start and end apart: 43, of which 18 were waited for; matrix products, arithmetic and copies ran while one was open for 1% of the time, Pallas kernels for 0%

commit v1 on v0

--- a/solution.py
+++ b/solution.py
@@ -89,7 +89,7 @@
 
 
 def precond_total(residual, precond):
-    return lax.psum(local_dots(residual, precond), ("tile", "level"))
+    return lax.psum(lax.psum(local_dots(residual, precond), "level"), "tile")
 
 
 def conjugate_solve(right_side, apply_q, apply_m):

time: 1670 us -> 1460 us (0.87)
  blocking collectives: 1120 us -> 937 us
  waiting for transfers between devices: 323 us -> 287 us
    psum x4 -> x8, blocking collectives: 607 us -> 260 us  [precond_total(): return lax.psum(lax.psum(local_dots(residual, precond), 'level'), 'tile')]
    psum x3 -> x4, blocking collectives: 451 us -> 615 us  [conjugate_solve(): curv_total = lax.psum(local_dots(direction, image_field), ('tile', 'level'))]
    unnamed x2, waiting for transfers between devices: 276 us -> 242 us
where the time goes in v1:
time: 1460 us; the launch traced here: 1450 us
  blocking collectives  937 us (64%)
  waiting for transfers between devices  287 us (20%)
  starting transfers between devices  101 us (7%)
  local copies, waits for them, and re-layouts  52.3 us (4%)
  other arithmetic  43.2 us (3%)
  between operations  24.5 us (2%)
    psum x4, blocking collectives, conjugate_solve(): curv_total = lax.psum(local_dots(direction, image_field), ('tile', 'level'))  615 us
    psum x8, blocking collectives, precond_total(): return lax.psum(lax.psum(local_dots(residual, precond), 'level'), 'tile')  260 us
    unnamed x2, waiting for transfers between devices  242 us
    ppermute x20, starting transfers between devices, with_halo(): lax.ppermute(tail, axis, [(i, (i + 1) % count) for i in range(ends)])  65.9 us
    unnamed x72, local copies, waits for them, and re-layouts  33.4 us
    all_to_all x4, blocking collectives, solve_columns(): lax.all_to_all(solved, 'level', split_axis=1, concat_axis=3, tiled=True)  32.7 us
    ppermute x20, waiting for transfers between devices, with_halo(): lax.ppermute(head, axis, [((i + 1) % count, i) for i in range(ends)])  31.3 us
    all_to_all x3, blocking collectives, apply_m(): lax.all_to_all(values, 'level', split_axis=3, concat_axis=1, tiled=True)  29.9 us
  transfers between devices with their start and end apart: 43, of which 18 were waited for; matrix products, arithmetic and copies ran while one was open for 1% of the time, Pallas kernels for 0%

profile of v1, /device:TPU:1, one launch (start us, length us, event | category | flops | bytes accessed | tf_op | source)
XLA Modules:
  0.0 1445.1 jit_solution(16941950590230095580)
XLA Ops:
  9.2 5.0 all-to-all-start.1
  33.5 8.0 all_to_all.165
  51.2 4.7 collective-permute-done.3
  66.3 4.7 collective-permute-done.7
  73.2 5.9 psum.84
  79.1 65.5 %psum.85 = f32[1]{0:T(128)} all-reduce(f32[1]{0:T(128)} %psum.84), channel_id=1, replica_groups=mesh['probe'=4,'tile'=32,'level'=2] {'tile'}, use_global_device_ids=true, to_apply=%region_2.3 | all-reduce | flops 1 | bytes 8 | tf_op jit(solution)/shard_map/psum | solution.py:92
  144.6 150.1 %psum.86 = f32[1]{0:T(128)} all-reduce(f32[1]{0:T(128)} %bitcast.30), channel_id=1, replica_groups=mesh['probe'=4,'tile'=32,'level'=2] {'tile','level'}, use_global_device_ids=true, to_apply=%region_4.5 | all-reduce | flops 1 | bytes 8 | tf_op jit(solution)/shard_map/psum | solution.py:104
  302.3 10.2 all_to_all.166
  323.0 8.3 all_to_all.167
  332.1 6.0 psum.87
  338.0 56.3 %psum.88 = f32[1]{0:T(128)} all-reduce(f32[1]{0:T(128)} %psum.87), channel_id=1, replica_groups=mesh['probe'=4,'tile'=32,'level'=2] {'tile'}, use_global_device_ids=true, to_apply=%region_7.8 | all-reduce | flops 1 | bytes 8 | tf_op jit(solution)/shard_map/psum | solution.py:92
  406.5 4.7 collective-permute-done.11
  422.3 4.7 collective-permute-done.15
  429.2 150.2 %psum.89 = f32[1]{0:T(128)} all-reduce(f32[1]{0:T(128)} %bitcast.43), channel_id=1, replica_groups=mesh['probe'=4,'tile'=32,'level'=2] {'tile','level'}, use_global_device_ids=true, to_apply=%region_9.10 | all-reduce | flops 1 | bytes 8 | tf_op jit(solution)/shard_map/psum | solution.py:104
  587.1 9.8 all_to_all.168
  607.4 8.0 all_to_all.169
  616.8 6.3 psum.90
  623.1 57.0 %psum.91 = f32[1]{0:T(128)} all-reduce(f32[1]{0:T(128)} %psum.90), channel_id=1, replica_groups=mesh['probe'=4,'tile'=32,'level'=2] {'tile'}, use_global_device_ids=true, to_apply=%region_12.13 | all-reduce | flops 1 | bytes 8 | tf_op jit(solution)/shard_map/psum | solution.py:92
  692.0 4.7 collective-permute-done.19
  707.2 4.7 collective-permute-done.23
  714.0 151.3 %psum.92 = f32[1]{0:T(128)} all-reduce(f32[1]{0:T(128)} %bitcast.56), channel_id=1, replica_groups=mesh['probe'=4,'tile'=32,'level'=2] {'tile','level'}, use_global_device_ids=true, to_apply=%region_14.15 | all-reduce | flops 1 | bytes 8 | tf_op jit(solution)/shard_map/psum | solution.py:104
  873.1 9.9 all_to_all.170
  893.5 8.4 all_to_all.171
  902.6 5.9 psum.93
  908.5 57.2 %psum.94 = f32[1]{0:T(128)} all-reduce(f32[1]{0:T(128)} %psum.93), channel_id=1, replica_groups=mesh['probe'=4,'tile'=32,'level'=2] {'tile'}, use_global_device_ids=true, to_apply=%region_17.18 | all-reduce | flops 1 | bytes 8 | tf_op jit(solution)/shard_map/psum | solution.py:92
  977.8 4.3 collective-permute-start.33
  989.3 5.6 collective-permute-start.30
  996.3 5.5 collective-permute-start.34
  1004.6 162.9 %psum.95 = f32[1]{0:T(128)} all-reduce(f32[1]{0:T(128)} %bitcast.69), channel_id=1, replica_groups=mesh['probe'=4,'tile'=32,'level'=2] {'tile','level'}, use_global_device_ids=true, to_apply=%region_19.20 | all-reduce | flops 1 | bytes 8 | tf_op jit(solution)/shard_map/psum | solution.py:104
  1183.9 4.3 copy.71
  1188.3 4.7 reshape.177
  1193.0 242.2 %reduce-scatter.4.cloned.1.call-done = f32[64,256]{1,0:T(8,128)} async-done(((f32[256,256]{1,0:T(8,128)}), f32[64,256]{1,0:T(8,128)}) %reduce-scatter.4.cloned.1.call-update) | async-done | bytes 65552
  (280 shorter events, 183.7 us)
Async XLA Ops:
  9.2 10.5 all-to-all-start.1
  19.7 9.0 all-to-all-start
  23.1 1412.1 %reduce-scatter.4.cloned.1.call-start = ((), (), s32[]{:S(2)}) async-start(), calls=%async_computation.10 | async-start | bytes 327680
  41.6 5.3 collective-permute-start
  49.8 6.0 collective-permute-start.3
  56.7 5.6 collective-permute-start.4
  58.0 5.3 collective-permute-start.5
  65.0 6.0 collective-permute-start.7
  396.7 5.4 collective-permute-start.8
  398.0 5.1 collective-permute-start.9
  405.2 6.0 collective-permute-start.11
  412.8 5.6 collective-permute-start.12
  414.1 5.3 collective-permute-start.13
  421.0 6.0 collective-permute-start.15
  682.6 5.5 collective-permute-start.16
  683.9 5.2 collective-permute-start.17
  690.7 6.0 collective-permute-start.19
  697.6 5.6 collective-permute-start.20
  698.9 5.3 collective-permute-start.21
  705.9 6.0 collective-permute-start.23
  967.2 5.3 collective-permute-start.24
  973.5 8.6 collective-permute-start.26
  975.1 7.0 collective-permute-start.27
  976.5 19.8 %collective-permute-start.32 = (f32[2,32,1,256]{3,2,1,0:T(1,128)S(1)}, f32[2,32,1,256]{3,2,1,0:T(1,128)S(1)}, u32[]{:S(2)}, u32[]{:S(2)}) collective-permute-start(f32[2,32,1,256]{3,2,1,0:T(1,128)S(1)} %get-tuple-element.45), channel_id=1, source_target_pairs={{2,0},{4,2},{6,4},{8,6},{10,8},{12,10},{14,12},{16,14},{18,16},{20... | collective-permute-start | bytes 196616 | tf_op jit(solution)/shard_map/ppermute | solution.py:20
  977.8 18.5 %collective-permute-start.33 = (f32[2,32,1,256]{3,2,1,0:T(1,128)S(1)}, f32[2,32,1,256]{3,2,1,0:T(1,128)S(1)}, u32[]{:S(2)}, u32[]{:S(2)}) collective-permute-start(f32[2,32,1,256]{3,2,1,0:T(1,128)S(1)} %get-tuple-element.44), channel_id=1, source_target_pairs={{0,2},{2,4},{4,6},{6,8},{8,10},{10,12},{12,14},{14,16},{16,18},{18... | collective-permute-start | bytes 196616 | tf_op jit(solution)/shard_map/ppermute | solution.py:18
  983.0 6.0 collective-permute-start.28
  989.3 13.8 collective-permute-start.30
  995.0 8.2 collective-permute-start.31
  996.3 178.1 %collective-permute-start.34 = (f32[2,1,10,256]{3,2,1,0:T(8,128)S(1)}, f32[2,1,10,256]{3,2,1,0:T(8,128)S(1)}, u32[]{:S(2)}, u32[]{:S(2)}) collective-permute-start(f32[2,1,10,256]{3,2,1,0:T(8,128)S(1)} %get-tuple-element.37), channel_id=1, source_target_pairs={{0,1},{2,3},{4,5},{6,7},{8,9},{10,11},{12,13},{14,15},{16,17},{18,... | collective-permute-start | bytes 61448 | tf_op jit(solution)/shard_map/ppermute | solution.py:18
  1001.8 172.7 %collective-permute-start.35 = (f32[2,1,10,256]{3,2,1,0:T(8,128)S(1)}, f32[2,1,10,256]{3,2,1,0:T(8,128)S(1)}, u32[]{:S(2)}, u32[]{:S(2)}) collective-permute-start(f32[2,1,10,256]{3,2,1,0:T(8,128)S(1)} %get-tuple-element.36), channel_id=1, source_target_pairs={{1,0},{3,2},{5,4},{7,6},{9,8},{11,10},{13,12},{15,14},{17,16},{19,... | collective-permute-start | bytes 61448 | tf_op jit(solution)/shard_map/ppermute | solution.py:20
  1169.0 6.5 collective-permute-start.36
  1176.9 6.1 collective-permute-start.39
  (39 other events, 841.5 us)
Sparse Core Ops, SparseCore 0:
  1193.1 242.0 reduce-scatter.3
